TPU v7x, 32 devices: a whole 2x2x4 slice. The times are simulated.
32 devices in a mesh: ctx: 16 (over z, x, core), head: 2 (over y).
Axes of the slice: x: 2, y: 2, z: 4, core: 2. Of those that a mesh axis runs over, the one named last changes fastest.
Arguments:
- q_absorbed: bfloat16 [2048, 64, 576], P('ctx', 'head'), may hold values from -6 to 6
- grad_out: bfloat16 [2048, 64, 512], P('ctx', 'head'), may hold values from -6 to 6
- log_norm: float32 [2048, 64], P('ctx', 'head'), may hold values from 5 to 7
- out_dot: float32 [2048, 64], P('ctx', 'head'), may hold values from -6 to 6
- kv_cache: bfloat16 [2048, 576], P(('ctx', 'head')), may hold values from -6 to 6
- block_links: int32 [16, 4], P('ctx'), may hold values 0 or 1
Outputs:
- d_query: bfloat16 [2048, 64, 576], P('ctx', 'head')
- d_kv: bfloat16 [2048, 576], P(('ctx', 'head'))
All inputs are finite; a program needn't handle non-finite values. No bound on the sum of `block_links` on one device may be relied on, other than what follows from the above.
Results may differ from a plain program's by a relative error of at most 0.0061.
Values may be sent and summed in bfloat16 or wider, within the bound.
A program may use at most 128 MiB of HBM per device.

v0:
```python
import functools
import math

import jax
import jax.numpy as jnp
from jax import lax
from jax.experimental import pallas as pl
from jax.experimental.pallas import tpu as pltpu
from jax.sharding import PartitionSpec as P

offset_list = (0, 1, 2, 8)
F32 = jnp.float32
BF16 = jnp.bfloat16


def dot(a, b, ca, cb):
    return lax.dot_general(a, b, (((ca,), (cb,)), ((), ())), preferred_element_type=F32)


def compute_kernel(heads, links, kv_ref, q_ref, g_ref, ln_ref, od_ref, dq_ref, dkv_ref, acc):
    step = pl.program_id(0)
    rows, feat = q_ref.shape
    lat = g_ref.shape[1]
    scale = feat ** (-0.5)
    log2e = math.log2(math.e)
    q = q_ref[...]
    g = g_ref[...]
    ln = ln_ref[...] * log2e
    od = od_ref[...]
    n_off, blk, _ = kv_ref.shape
    kv = kv_ref[...].reshape(n_off * blk, feat)
    s = dot(kv, q, 1, 1)
    dp = dot(kv[:, :lat], g, 1, 1)
    ps, dss = [], []
    for pos in range(n_off):
        sl = slice(pos * blk, (pos + 1) * blk)
        bias = jnp.where(links[0, pos] > 0, ln, 1e30)
        p = jnp.exp2(s[sl] * (scale * log2e) - bias)
        if offset_list[pos] == 0:
            key = lax.broadcasted_iota(jnp.int32, p.shape, 0)
            row = lax.broadcasted_iota(jnp.int32, p.shape, 1) + step * rows
            p = jnp.where(row >= key * heads, p, 0.0)
        ps.append(p.astype(BF16))
        dss.append((p * (dp[sl] - od) * scale).astype(BF16))
    pb = jnp.concatenate(ps, 0)
    ds = jnp.concatenate(dss, 0)
    dq_ref[...] = dot(ds, kv, 0, 0).astype(BF16)
    dk = dot(ds, q, 1, 0)
    dv = dot(pb, g, 1, 0)

    @pl.when(step == 0)
    def _():
        acc[...] = jnp.zeros_like(acc)

    acc[:, :lat] += dk[:, :lat] + dv
    acc[:, lat:] += dk[:, lat:]

    @pl.when(step == pl.num_programs(0) - 1)
    def _():
        dkv_ref[...] = acc[...].astype(dkv_ref.dtype).reshape(dkv_ref.shape)


def compute(q, g, ln, od, kv, links, tile=512):
    toks, heads, feat = q.shape
    lat = g.shape[2]
    rows = toks * heads
    n_off, blk, _ = kv.shape
    tile = min(tile, rows)
    dq, dkv = pl.pallas_call(
        functools.partial(compute_kernel, heads),
        grid=(rows // tile,),
        in_specs=[
            pl.BlockSpec(memory_space=pltpu.SMEM),
            pl.BlockSpec((n_off, blk, feat), lambda i: (0, 0, 0)),
            pl.BlockSpec((tile, feat), lambda i: (i, 0)),
            pl.BlockSpec((tile, lat), lambda i: (i, 0)),
            pl.BlockSpec((1, tile), lambda i: (0, i)),
            pl.BlockSpec((1, tile), lambda i: (0, i)),
        ],
        out_specs=[
            pl.BlockSpec((tile, feat), lambda i: (i, 0)),
            pl.BlockSpec((n_off, blk, feat), lambda i: (0, 0, 0)),
        ],
        out_shape=[
            jax.ShapeDtypeStruct((rows, feat), BF16),
            jax.ShapeDtypeStruct((n_off, blk, feat), F32),
        ],
        scratch_shapes=[pltpu.VMEM((n_off * blk, feat), F32)],
        compiler_params=pltpu.CompilerParams(dimension_semantics=("arbitrary",), vmem_limit_bytes=48 << 20),
        name="mla_bwd",
    )(links, kv, q.reshape(rows, feat), g.reshape(rows, lat), ln.reshape(1, rows), od.reshape(1, rows))
    return dq.reshape(toks, heads, feat), dkv


def from_behind(array, axis, by):
    length = lax.axis_size(axis)
    return lax.ppermute(array, axis, [(i, (i + by) % length) for i in range(length)])


def shards(q, g, ln, od, kv, links):
    own = lax.all_gather(kv, "head", axis=0, tiled=True)
    keys = jnp.stack([own] + [from_behind(own, "ctx", o) for o in offset_list[1:]])
    dq, part = compute(q, g, ln, od, keys, links)
    total = part[0]
    for pos in range(1, len(offset_list)):
        total = total + from_behind(part[pos].astype(BF16), "ctx", -offset_list[pos]).astype(F32)
    dkv = lax.psum_scatter(total, "head", scatter_dimension=0, tiled=True)
    return dq, dkv.astype(BF16)


def solution(mesh):
    in_specs = (
        P("ctx", "head", None),
        P("ctx", "head", None),
        P("ctx", "head"),
        P("ctx", "head"),
        P(("ctx", "head"), None),
        P("ctx", None),
    )
    out_specs = (P("ctx", "head", None), P(("ctx", "head"), None))
    return jax.shard_map(shards, mesh=mesh, in_specs=in_specs, out_specs=out_specs, check_vma=False)
```

profile of v0, /device:TPU:0, one launch (start us, length us, event | category | flops | bytes accessed | tf_op | source)
XLA Modules:
  0.0 90.0 jit_solution(7206691290035667294)
XLA Ops:
  7.2 0.0 reduce-scatter.2.cloned.1.call-start
  7.2 6.4 %all_gather.3 = bf16[128,576]{1,0:T(8,128)(2,1)S(1)} all-gather(bf16[64,576]{1,0:T(8,128)(2,1)} %param.10), channel_id=1, replica_groups=mesh['ctx'=16,'head'=2] {'head'}, dimensions={0}, use_global_device_ids=true | all-gather | bytes 221184 | tf_op jit(solution)/shard_map/all_gather | solution.py:101
  13.6 3.0 %collective-permute-start.2 = (bf16[128,576]{1,0:T(8,128)(2,1)S(1)}, bf16[128,576]{1,0:T(8,128)(2,1)S(1)}, u32[]{:S(2)}, u32[]{:S(2)}) collective-permute-start(bf16[128,576]{1,0:T(8,128)(2,1)S(1)} %all_gather.3), channel_id=1, source_target_pairs={{0,16},{2,18},{4,20},{6,22},{8,24},{10,26},{12,28},{14,30},{16,0},... | collective-permute-start | bytes 442376 | tf_op jit(solution)/shard_map/ppermute | solution.py:97
  16.6 1.5 %collective-permute-start.1 = (bf16[128,576]{1,0:T(8,128)(2,1)S(1)}, bf16[128,576]{1,0:T(8,128)(2,1)S(1)}, u32[]{:S(2)}, u32[]{:S(2)}) collective-permute-start(bf16[128,576]{1,0:T(8,128)(2,1)S(1)} %all_gather.3), channel_id=1, source_target_pairs={{0,4},{2,6},{4,8},{6,10},{8,12},{10,14},{12,16},{14,18},{16,20},{1... | collective-permute-start | bytes 442376 | tf_op jit(solution)/shard_map/ppermute | solution.py:97
  18.1 0.0 collective-permute-start
  18.1 0.8 copy.13
  18.9 0.1 reshape.24.ln_ref
  19.0 0.8 copy.14
  19.8 0.1 reshape.25.od_ref
  19.9 0.0 copy-start.1
  19.9 9.0 %copy.12 = bf16[128,32,576]{2,1,0:T(8,128)(2,1)} copy(bf16[128,32,576]{0,2,1:T(8,128)(2,1)} %param.6) | data formatting | bytes 9437184 | tf_op args[0]
  28.9 0.0 collective-permute-done.2
  28.9 0.0 collective-permute-done.1
  28.9 0.0 collective-permute-done
  28.9 0.1 pad_maximum_fusion.kv_ref
  29.1 0.0 copy-done.1
  29.1 0.0 copy-start
  29.1 2.2 %copy-done = bf16[128,32,512]{2,1,0:T(8,128)(2,1)S(1)} copy-done((bf16[128,32,512]{2,1,0:T(8,128)(2,1)S(1)}, bf16[128,32,512]{2,1,0:T(8,128)(2,1)}, u32[]{:S(2)}) %copy-start) | copy-done | bytes 4194328
  31.3 20.2 %mla_bwd.1 = (bf16[4096,576]{1,0:T(8,128)(2,1)}, f32[4,128,576]{2,1,0:T(8,128)S(1)}) custom-call(s32[1,4]{1,0:T(1,128)S(1)} %copy-done.1, bf16[4,128,576]{2,1,0:T(8,128)(2,1)S(1)} %pad_maximum_fusion.kv_ref, bf16[4096,576]{1,0:T(8,128)(2,1)} %bitcast.20, bf16[4096,512]{1,0:T(8,128)(2,1)S(1)} %bitcast.19, f32[1,4096]{1,0:T(1,128)S(1)} %reshape.24.ln_ref, ...), custom_call_target="tpu_custom_call" | custom-call | tf_op jit(solution)/shard_map/mla_bwd/pallas_call | solution.py:69
  51.4 0.1 convert.5
  51.6 4.5 %collective-permute-start.3 = (bf16[128,576]{1,0:T(8,128)(2,1)S(1)}, bf16[128,576]{1,0:T(8,128)(2,1)S(1)}, u32[]{:S(2)}, u32[]{:S(2)}) collective-permute-start(bf16[128,576]{1,0:T(8,128)(2,1)S(1)} %get-tuple-element.10), channel_id=1, source_target_pairs={{0,30},{2,0},{4,2},{6,4},{8,6},{10,8},{12,10},{14,12},{16,14},{18,... | collective-permute-start | bytes 442376 | tf_op jit(solution)/shard_map/ppermute | solution.py:97
  56.1 0.0 collective-permute-start.5
  56.1 0.7 collective-permute-start.4
  56.8 3.9 %collective-permute-done.3 = bf16[128,576]{1,0:T(8,128)(2,1)S(1)} collective-permute-done((bf16[128,576]{1,0:T(8,128)(2,1)S(1)}, bf16[128,576]{1,0:T(8,128)(2,1)S(1)}, u32[]{:S(2)}, u32[]{:S(2)}) %collective-permute-start.3) | collective-permute-done | bytes 147488 | tf_op jit(solution)/shard_map/ppermute | solution.py:97
  60.7 5.6 %collective-permute-done.5 = bf16[128,576]{1,0:T(8,128)(2,1)S(1)} collective-permute-done((bf16[128,576]{1,0:T(8,128)(2,1)S(1)}, bf16[128,576]{1,0:T(8,128)(2,1)S(1)}, u32[]{:S(2)}, u32[]{:S(2)}) %collective-permute-start.5) | collective-permute-done | bytes 147488 | tf_op jit(solution)/shard_map/ppermute | solution.py:97
  66.3 0.0 collective-permute-done.4
  66.3 0.8 fusion.1
  67.1 0.0 reduce-scatter.2.cloned.1.call-update
  67.1 8.6 %copy.15 = bf16[128,32,576]{0,2,1:T(8,128)(2,1)} copy(bf16[128,32,576]{2,1,0:T(8,128)(2,1)} %bitcast.21) | data formatting | bytes 9437184
  75.7 5.9 %reduce-scatter.2.cloned.1.call-done = f32[64,576]{1,0:T(8,128)} async-done(((f32[128,576]{1,0:T(8,128)}), f32[64,576]{1,0:T(8,128)}) %reduce-scatter.2.cloned.1.call-update) | async-done | bytes 147472 | tf_op jit(solution)/shard_map/reduce_scatter | solution.py:107
  81.6 1.6 %convert_element_type.30 = bf16[64,576]{1,0:T(8,128)(2,1)} convert(f32[64,576]{1,0:T(8,128)} %reduce-scatter.2.cloned.1.call-done) | non-fusion elementwise | flops 36864 | bytes 221184 | tf_op jit(solution)/shard_map/convert_element_type | solution.py:108
  (1 shorter events, 0.0 us)
Async XLA Ops:
  7.2 74.4 %reduce-scatter.2.cloned.1.call-start = ((), (), s32[]{:S(2)}) async-start(), calls=%async_computation.1 | async-start | bytes 491520 | tf_op jit(solution)/shard_map/reduce_scatter | solution.py:107
  13.6 15.3 %collective-permute-start.2 = (bf16[128,576]{1,0:T(8,128)(2,1)S(1)}, bf16[128,576]{1,0:T(8,128)(2,1)S(1)}, u32[]{:S(2)}, u32[]{:S(2)}) collective-permute-start(bf16[128,576]{1,0:T(8,128)(2,1)S(1)} %all_gather.3), channel_id=1, source_target_pairs={{0,16},{2,18},{4,20},{6,22},{8,24},{10,26},{12,28},{14,30},{16,0},... | collective-permute-start | bytes 442376 | tf_op jit(solution)/shard_map/ppermute | solution.py:97
  16.6 12.3 %collective-permute-start.1 = (bf16[128,576]{1,0:T(8,128)(2,1)S(1)}, bf16[128,576]{1,0:T(8,128)(2,1)S(1)}, u32[]{:S(2)}, u32[]{:S(2)}) collective-permute-start(bf16[128,576]{1,0:T(8,128)(2,1)S(1)} %all_gather.3), channel_id=1, source_target_pairs={{0,4},{2,6},{4,8},{6,10},{8,12},{10,14},{12,16},{14,18},{16,20},{1... | collective-permute-start | bytes 442376 | tf_op jit(solution)/shard_map/ppermute | solution.py:97
  18.1 10.8 %collective-permute-start = (bf16[128,576]{1,0:T(8,128)(2,1)S(1)}, bf16[128,576]{1,0:T(8,128)(2,1)S(1)}, u32[]{:S(2)}, u32[]{:S(2)}) collective-permute-start(bf16[128,576]{1,0:T(8,128)(2,1)S(1)} %all_gather.3), channel_id=1, source_target_pairs={{0,2},{2,4},{4,6},{6,8},{8,10},{10,12},{12,14},{14,16},{16,18},{18... | collective-permute-start | bytes 442376 | tf_op jit(solution)/shard_map/ppermute | solution.py:97
  19.9 9.1 %copy-start.1 = (s32[1,4]{1,0:T(1,128)S(1)}, s32[1,4]{1,0:T(1,128)}, u32[]{:S(2)}) copy-start(s32[1,4]{1,0:T(1,128)} %links.1) | copy-start | bytes 52
  29.1 2.2 %copy-start = (bf16[128,32,512]{2,1,0:T(8,128)(2,1)S(1)}, bf16[128,32,512]{2,1,0:T(8,128)(2,1)}, u32[]{:S(2)}) copy-start(bf16[128,32,512]{2,1,0:T(8,128)(2,1)} %param.7) | copy-start | bytes 12582916
  51.6 9.1 %collective-permute-start.3 = (bf16[128,576]{1,0:T(8,128)(2,1)S(1)}, bf16[128,576]{1,0:T(8,128)(2,1)S(1)}, u32[]{:S(2)}, u32[]{:S(2)}) collective-permute-start(bf16[128,576]{1,0:T(8,128)(2,1)S(1)} %get-tuple-element.10), channel_id=1, source_target_pairs={{0,30},{2,0},{4,2},{6,4},{8,6},{10,8},{12,10},{14,12},{16,14},{18,... | collective-permute-start | bytes 442376 | tf_op jit(solution)/shard_map/ppermute | solution.py:97
  56.1 10.2 %collective-permute-start.5 = (bf16[128,576]{1,0:T(8,128)(2,1)S(1)}, bf16[128,576]{1,0:T(8,128)(2,1)S(1)}, u32[]{:S(2)}, u32[]{:S(2)}) collective-permute-start(bf16[128,576]{1,0:T(8,128)(2,1)S(1)} %get-tuple-element.11), channel_id=1, source_target_pairs={{0,16},{2,18},{4,20},{6,22},{8,24},{10,26},{12,28},{14,30},{16,0},... | collective-permute-start | bytes 442376 | tf_op jit(solution)/shard_map/ppermute | solution.py:97
  56.1 10.2 %collective-permute-start.4 = (bf16[128,576]{1,0:T(8,128)(2,1)S(1)}, bf16[128,576]{1,0:T(8,128)(2,1)S(1)}, u32[]{:S(2)}, u32[]{:S(2)}) collective-permute-start(bf16[128,576]{1,0:T(8,128)(2,1)S(1)} %get-tuple-element.12), channel_id=1, source_target_pairs={{0,28},{2,30},{4,0},{6,2},{8,4},{10,6},{12,8},{14,10},{16,12},{18,... | collective-permute-start | bytes 442376 | tf_op jit(solution)/shard_map/ppermute | solution.py:97
Sparse Core Ops, SparseCore 0:
  67.2 14.3 reduce-scatter.1
where the time goes:
time: 90.7 us; the launch traced here: 90 us
  local copies, waits for them, and re-layouts  21.6 us (24%)
  Pallas kernels  20.2 us (22%)
  waiting for transfers between devices  15.4 us (17%)
  between operations  14.1 us (16%)
  starting transfers between devices  9.73 us (11%)
  blocking collectives  6.37 us (7%)
  other arithmetic  2.58 us (3%)
    unnamed x8, local copies, waits for them, and re-layouts  21.4 us
    pallas_call x1, Pallas kernels, compute(): pl.pallas_call(functools.partial(compute_kernel, heads), grid=(rows // ti...  20.2 us
    ppermute x6, starting transfers between devices, from_behind(): lax.ppermute(array, axis, [(i, (i + by) % length) for i in range(length)])  9.69 us
    ppermute x6, waiting for transfers between devices, from_behind(): lax.ppermute(array, axis, [(i, (i + by) % length) for i in range(length)])  9.52 us
    all_gather x1, blocking collectives, shards(): own = lax.all_gather(kv, 'head', axis=0, tiled=True)  6.37 us
    reduce_scatter x1, waiting for transfers between devices, shards(): dkv = lax.psum_scatter(total, 'head', scatter_dimension=0, tiled=True)  5.86 us
  transfers between devices with their start and end apart: 7, of which 3 were waited for; matrix products, arithmetic and copies ran while one was open for 22% of the time, Pallas kernels for 0%

commit v1 on v0

v1 whole, which is shorter than its diff:
```python
import functools
import math

import jax
import jax.numpy as jnp
from jax import lax
from jax.experimental import pallas as pl
from jax.experimental.pallas import tpu as pltpu
from jax.sharding import PartitionSpec as P

offset_list = (0, 1, 2, 8)
F32 = jnp.float32
BF16 = jnp.bfloat16


def dot(a, b, ca, cb):
    return lax.dot_general(a, b, (((ca,), (cb,)), ((), ())), preferred_element_type=F32)


def compute_kernel(n_head, head_at, links, kv_ref, q_ref, g_ref, ln_ref, od_ref, dq_ref, own_ref, away_ref, acc):
    step = pl.program_id(0)
    group, feat, toks = q_ref.shape
    lat = g_ref.shape[2]
    scale = feat ** (-0.5)
    log2e = math.log2(math.e)
    cols = group * toks
    q = jnp.concatenate([q_ref[i] for i in range(group)], 1)
    g = g_ref[...].reshape(cols, lat)
    ln = jnp.concatenate([ln_ref[0, i : i + 1, :] for i in range(group)], 1) * log2e
    od = jnp.concatenate([od_ref[0, i : i + 1, :] for i in range(group)], 1)
    n_off, _, part, _ = kv_ref.shape
    blk = n_head * part
    kv = kv_ref[...].reshape(n_off * blk, feat)
    s = dot(kv, q, 1, 0)
    dp = dot(kv[:, :lat], g, 1, 1)
    ps, dss = [], []
    for pos in range(n_off):
        sl = slice(pos * blk, (pos + 1) * blk)
        bias = jnp.where(links[0, pos] > 0, ln, 1e30)
        p = jnp.exp2(s[sl] * (scale * log2e) - bias)
        if offset_list[pos] == 0:
            key = lax.broadcasted_iota(jnp.int32, p.shape, 0) + head_at[0] * part
            key = jnp.where(key >= blk, key - blk, key)
            tok = lax.rem(lax.broadcasted_iota(jnp.int32, p.shape, 1), toks)
            p = jnp.where(tok >= key, p, 0.0)
        ps.append(p.astype(BF16))
        dss.append((p * (dp[sl] - od) * scale).astype(BF16))
    pb = jnp.concatenate(ps, 0)
    ds = jnp.concatenate(dss, 0)
    dq = dot(kv, ds, 0, 0).astype(BF16)
    for i in range(group):
        dq_ref[i] = dq[:, i * toks : (i + 1) * toks]
    dk = dot(ds, q, 1, 1)
    dv = dot(pb, g, 1, 0)

    @pl.when(step == 0)
    def _():
        acc[...] = jnp.zeros_like(acc)

    acc[:, :lat] += dk[:, :lat] + dv
    acc[:, lat:] += dk[:, lat:]

    @pl.when(step == pl.num_programs(0) - 1)
    def _():
        total = acc[...].reshape(n_off, n_head, part, feat)
        own_ref[...] = total[:, 0]
        away_ref[...] = total[:, 1:].astype(BF16)


def compute(n_head, q, g, ln, od, kv, links, group=4):
    heads, feat, toks = q.shape
    lat = g.shape[2]
    n_off, _, part, _ = kv.shape
    group = math.gcd(group, heads)
    steps = heads // group
    head_at = lax.axis_index("head").astype(jnp.int32).reshape(1)
    return pl.pallas_call(
        functools.partial(compute_kernel, n_head),
        grid=(steps,),
        in_specs=[
            pl.BlockSpec(memory_space=pltpu.SMEM),
            pl.BlockSpec(memory_space=pltpu.SMEM),
            pl.BlockSpec(kv.shape, lambda i: (0, 0, 0, 0)),
            pl.BlockSpec((group, feat, toks), lambda i: (i, 0, 0)),
            pl.BlockSpec((group, toks, lat), lambda i: (i, 0, 0)),
            pl.BlockSpec((1, group, toks), lambda i: (i, 0, 0)),
            pl.BlockSpec((1, group, toks), lambda i: (i, 0, 0)),
        ],
        out_specs=[
            pl.BlockSpec((group, feat, toks), lambda i: (i, 0, 0)),
            pl.BlockSpec((n_off, part, feat), lambda i: (0, 0, 0)),
            pl.BlockSpec((n_off, n_head - 1, part, feat), lambda i: (0, 0, 0, 0)),
        ],
        out_shape=[
            jax.ShapeDtypeStruct((heads, feat, toks), BF16),
            jax.ShapeDtypeStruct((n_off, part, feat), F32),
            jax.ShapeDtypeStruct((n_off, n_head - 1, part, feat), BF16),
        ],
        scratch_shapes=[pltpu.VMEM((n_off * n_head * part, feat), F32)],
        compiler_params=pltpu.CompilerParams(dimension_semantics=("arbitrary",), vmem_limit_bytes=48 << 20),
        cost_estimate=pl.CostEstimate(flops=12 * 10**9, bytes_accessed=14 * 10**6, transcendentals=2 * 10**6),
        name="mla_bwd",
    )(head_at, links, kv, q, g, ln.reshape(steps, group, toks), od.reshape(steps, group, toks))


def from_behind(array, axis, by):
    length = lax.axis_size(axis)
    return lax.ppermute(array, axis, [(i, (i + by) % length) for i in range(length)])


def shards(q, g, ln, od, kv, links):
    n_head = lax.axis_size("head")
    mine = [kv] + [from_behind(kv, "ctx", o) for o in offset_list[1:]]
    keys = jnp.stack([jnp.stack([m] + [from_behind(m, "head", -j) for j in range(1, n_head)]) for m in mine])
    dq, own, away = compute(
        n_head,
        jnp.transpose(q, (1, 2, 0)),
        jnp.transpose(g, (1, 0, 2)),
        ln.T,
        od.T,
        keys,
        links,
    )
    for j in range(1, n_head):
        own = own + from_behind(away[:, j - 1], "head", j).astype(F32)
    total = own[0]
    for pos in range(1, len(offset_list)):
        total = total + from_behind(own[pos].astype(BF16), "ctx", -offset_list[pos]).astype(F32)
    return jnp.transpose(dq, (2, 0, 1)), total.astype(BF16)


def solution(mesh):
    in_specs = (
        P("ctx", "head", None),
        P("ctx", "head", None),
        P("ctx", "head"),
        P("ctx", "head"),
        P(("ctx", "head"), None),
        P("ctx", None),
    )
    out_specs = (P("ctx", "head", None), P(("ctx", "head"), None))
    return jax.shard_map(shards, mesh=mesh, in_specs=in_specs, out_specs=out_specs, check_vma=False)
```

time: 90.7 us -> 58.7 us (0.65)
  local copies, waits for them, and re-layouts: 21.6 us -> 4.59 us
  between operations: 14.1 us -> 0.73 us
  blocking collectives: 6.37 us -> 0 us
  waiting for transfers between devices: 15.4 us -> 19.7 us
  starting transfers between devices: 9.73 us -> 13.6 us
  other arithmetic: 2.58 us -> 1.02 us
  Pallas kernels: 20.2 us -> 18.8 us
    unnamed x8 -> x9, local copies, waits for them, and re-layouts: 21.4 us -> 4.57 us
    ppermute x6 -> x11, waiting for transfers between devices: 9.52 us -> 19.7 us  [from_behind(): lax.ppermute(array, axis, [(i, (i + by) % length) for i in range(length)])]
    all_gather x1 -> x0, blocking collectives: 6.37 us -> none  [shards(): own = lax.all_gather(kv, 'head', axis=0, tiled=True)]
    reduce_scatter x1 -> x0, waiting for transfers between devices: 5.86 us -> none  [shards(): dkv = lax.psum_scatter(total, 'head', scatter_dimension=0, tiled=True)]
    ppermute x6 -> x11, starting transfers between devices: 9.69 us -> 13.6 us  [from_behind(): lax.ppermute(array, axis, [(i, (i + by) % length) for i in range(length)])]
    pallas_call x1, Pallas kernels: 20.2 us -> 18.8 us  [compute(): pl.pallas_call(functools.partial(compute_kernel, n_head), grid=(steps,),...]
  transfers between devices with their start and end apart: 7 -> 11, of which waited for: 3 -> 6; matrix products, arithmetic and copies ran while one was open for 22% -> 8% of each run, Pallas kernels for 0% -> 0%
where the time goes in v1:
time: 58.7 us; the launch traced here: 58.5 us
  waiting for transfers between devices  19.7 us (34%)
  Pallas kernels  18.8 us (32%)
  starting transfers between devices  13.6 us (23%)
  local copies, waits for them, and re-layouts  4.59 us (8%)
  other arithmetic  1.02 us (2%)
  between operations  0.73 us (1%)
    ppermute x11, waiting for transfers between devices, from_behind(): lax.ppermute(array, axis, [(i, (i + by) % length) for i in range(length)])  19.7 us
    pallas_call x1, Pallas kernels, compute(): pl.pallas_call(functools.partial(compute_kernel, n_head), grid=(steps,),...  18.8 us
    ppermute x11, starting transfers between devices, from_behind(): lax.ppermute(array, axis, [(i, (i + by) % length) for i in range(length)])  13.6 us
    unnamed x9, local copies, waits for them, and re-layouts  4.57 us
  transfers between devices with their start and end apart: 11, of which 6 were waited for; matrix products, arithmetic and copies ran while one was open for 8% of the time, Pallas kernels for 0%

profile of v1, /device:TPU:0, one launch (start us, length us, event | category | flops | bytes accessed | tf_op | source)
XLA Modules:
  0.0 58.5 jit_solution(992483829603691330)
XLA Ops:
  0.6 0.0 copy-start.3
  0.6 0.5 collective-permute-start.1
  1.2 3.7 %collective-permute-start.5 = (bf16[64,576]{1,0:T(8,128)(2,1)}, bf16[64,576]{1,0:T(8,128)(2,1)S(1)}, u32[]{:S(2)}, u32[]{:S(2)}) collective-permute-start(bf16[64,576]{1,0:T(8,128)(2,1)} %param.10), channel_id=1, source_target_pairs={{0,16},{2,18},{4,20},{6,22},{8,24},{10,26},{12,28},{14,30},{16,0},... | collective-permute-start | bytes 221192 | tf_op jit(solution)/shard_map/ppermute | solution.py:108
  4.8 1.5 %collective-permute-start.3 = (bf16[64,576]{1,0:T(8,128)(2,1)}, bf16[64,576]{1,0:T(8,128)(2,1)S(1)}, u32[]{:S(2)}, u32[]{:S(2)}) collective-permute-start(bf16[64,576]{1,0:T(8,128)(2,1)} %param.10), channel_id=1, source_target_pairs={{0,4},{2,6},{4,8},{6,10},{8,12},{10,14},{12,16},{14,18},{16,20},{1... | collective-permute-start | bytes 221192 | tf_op jit(solution)/shard_map/ppermute | solution.py:108
  6.3 1.5 %collective-permute-start = (bf16[64,576]{1,0:T(8,128)(2,1)}, bf16[64,576]{1,0:T(8,128)(2,1)S(1)}, u32[]{:S(2)}, u32[]{:S(2)}) collective-permute-start(bf16[64,576]{1,0:T(8,128)(2,1)} %param.10), channel_id=1, source_target_pairs={{0,1},{1,0},{2,3},{3,2},{4,5},{5,4},{6,7},{7,6},{8,9},{9,8},{10,11... | collective-permute-start | bytes 221192 | tf_op jit(solution)/shard_map/ppermute | solution.py:108
  7.9 4.6 %copy.10 = bf16[128,32,512]{2,0,1:T(8,128)(2,1)S(1)} copy(bf16[128,32,512]{2,1,0:T(8,128)(2,1)} %param.7) | data formatting | bytes 8388608 | tf_op args[1]
  12.4 0.0 collective-permute-done.1
  12.4 0.6 collective-permute-start.2
  13.0 0.0 collective-permute-done.5
  13.0 1.5 %collective-permute-start.6 = (bf16[64,576]{1,0:T(8,128)(2,1)S(1)}, bf16[64,576]{1,0:T(8,128)(2,1)S(1)}, u32[]{:S(2)}, u32[]{:S(2)}) collective-permute-start(bf16[64,576]{1,0:T(8,128)(2,1)S(1)} %collective-permute-done.5), channel_id=1, source_target_pairs={{0,1},{1,0},{2,3},{3,2},{4,5},{5,4},{6,7},{7,6},{8,9},{9,8},{10,11... | collective-permute-start | bytes 221192 | tf_op jit(solution)/shard_map/ppermute | solution.py:108
  14.5 0.0 collective-permute-done.3
  14.5 0.5 collective-permute-start.4
  15.0 0.0 collective-permute-done
  15.0 0.0 copy-done.3
  15.1 2.7 %collective-permute-done.2 = bf16[64,576]{1,0:T(8,128)(2,1)S(1)} collective-permute-done((bf16[64,576]{1,0:T(8,128)(2,1)S(1)}, bf16[64,576]{1,0:T(8,128)(2,1)S(1)}, u32[]{:S(2)}, u32[]{:S(2)}) %collective-permute-start.2) | collective-permute-done | bytes 73760 | tf_op jit(solution)/shard_map/ppermute | solution.py:108
  17.8 1.7 %collective-permute-done.6 = bf16[64,576]{1,0:T(8,128)(2,1)S(1)} collective-permute-done((bf16[64,576]{1,0:T(8,128)(2,1)S(1)}, bf16[64,576]{1,0:T(8,128)(2,1)S(1)}, u32[]{:S(2)}, u32[]{:S(2)}) %collective-permute-start.6) | collective-permute-done | bytes 73760 | tf_op jit(solution)/shard_map/ppermute | solution.py:108
  19.6 1.5 %collective-permute-done.4 = bf16[64,576]{1,0:T(8,128)(2,1)S(1)} collective-permute-done((bf16[64,576]{1,0:T(8,128)(2,1)S(1)}, bf16[64,576]{1,0:T(8,128)(2,1)S(1)}, u32[]{:S(2)}, u32[]{:S(2)}) %collective-permute-start.4) | collective-permute-done | bytes 73760 | tf_op jit(solution)/shard_map/ppermute | solution.py:108
  21.1 0.1 pad_maximum_fusion.kv_ref
  21.3 0.0 copy-done
  21.3 0.0 copy-done.1
  21.3 0.0 copy-done.2
  21.3 18.8 %mla_bwd.1 = (bf16[32,576,128]{2,1,0:T(8,128)(2,1)}, f32[4,64,576]{2,1,0:T(8,128)S(1)}, bf16[4,1,64,576]{3,2,1,0:T(8,128)(2,1)S(1)}) custom-call(s32[1]{0:T(128)} %bitcast.head_at, s32[1,4]{1,0:T(1,128)S(1)} %copy-done.2, bf16[4,2,64,576]{3,2,1,0:T(8,128)(2,1)S(1)} %pad_maximum_fusion.kv_ref, bf16[32,576,128]{2,1,0:T(8,128)(2,1)} %bitcast.57, ...), custom_call_target="tpu_custom_call" | custom-call | flops 12000000000 | bytes 14000000 | tf_op jit(solution)/shard_map/mla_bwd/pallas_call | solution.py:77
  40.1 0.5 collective-permute-start.7
  40.6 9.0 %collective-permute-done.7 = bf16[4,64,576]{2,1,0:T(8,128)(2,1)S(1)} collective-permute-done((bf16[4,64,576]{2,1,0:T(8,128)(2,1)S(1)}, bf16[4,64,576]{2,1,0:T(8,128)(2,1)S(1)}, u32[]{:S(2)}, u32[]{:S(2)}) %collective-permute-start.7) | collective-permute-done | bytes 294944 | tf_op jit(solution)/shard_map/ppermute | solution.py:108
  49.6 0.1 fusion.4
  49.8 1.8 %collective-permute-start.8 = (bf16[64,576]{1,0:T(8,128)(2,1)S(1)}, bf16[64,576]{1,0:T(8,128)(2,1)S(1)}, u32[]{:S(2)}, u32[]{:S(2)}) collective-permute-start(bf16[64,576]{1,0:T(8,128)(2,1)S(1)} %get-tuple-element.10), channel_id=1, source_target_pairs={{0,30},{2,0},{4,2},{6,4},{8,6},{10,8},{12,10},{14,12},{16,14},{18,... | collective-permute-start | bytes 221192 | tf_op jit(solution)/shard_map/ppermute | solution.py:108
  51.5 0.0 collective-permute-start.10
  51.5 1.6 %collective-permute-start.9 = (bf16[64,576]{1,0:T(8,128)(2,1)S(1)}, bf16[64,576]{1,0:T(8,128)(2,1)S(1)}, u32[]{:S(2)}, u32[]{:S(2)}) collective-permute-start(bf16[64,576]{1,0:T(8,128)(2,1)S(1)} %get-tuple-element.12), channel_id=1, source_target_pairs={{0,28},{2,30},{4,0},{6,2},{8,4},{10,6},{12,8},{14,10},{16,12},{18,... | collective-permute-start | bytes 221192 | tf_op jit(solution)/shard_map/ppermute | solution.py:108
  53.1 0.5 collective-permute-done.8
  53.6 4.2 %collective-permute-done.10 = bf16[64,576]{1,0:T(8,128)(2,1)S(1)} collective-permute-done((bf16[64,576]{1,0:T(8,128)(2,1)S(1)}, bf16[64,576]{1,0:T(8,128)(2,1)S(1)}, u32[]{:S(2)}, u32[]{:S(2)}) %collective-permute-start.10) | collective-permute-done | bytes 73760 | tf_op jit(solution)/shard_map/ppermute | solution.py:108
  57.8 0.0 collective-permute-done.9
  57.8 0.7 %fusion.3 = bf16[64,576]{1,0:T(8,128)(2,1)} fusion(f32[4,64,576]{2,1,0:T(8,128)S(1)} %get-tuple-element.9, bf16[64,576]{1,0:T(8,128)(2,1)S(1)} %collective-permute-done.10, bf16[64,576]{1,0:T(8,128)(2,1)S(1)} %collective-permute-done.9, bf16[64,576]{1,0:T(8,128)(2,1)S(1)} %collective-permute-done.8), kind=kLoop, calls=%fused_computation.7 | loop fusion | flops 258048 | bytes 442368 | tf_op jit(solution)/shard_map/convert_element_type | solution.py:129
  (8 shorter events, 0.1 us)
Async XLA Ops:
  0.6 14.4 %copy-start.3 = (bf16[64,576]{1,0:T(8,128)(2,1)S(1)}, bf16[64,576]{1,0:T(8,128)(2,1)}, u32[]{:S(2)}) copy-start(bf16[64,576]{1,0:T(8,128)(2,1)} %param.10) | copy-start | bytes 221188
  0.6 11.8 %collective-permute-start.1 = (bf16[64,576]{1,0:T(8,128)(2,1)}, bf16[64,576]{1,0:T(8,128)(2,1)S(1)}, u32[]{:S(2)}, u32[]{:S(2)}) collective-permute-start(bf16[64,576]{1,0:T(8,128)(2,1)} %param.10), channel_id=1, source_target_pairs={{0,2},{2,4},{4,6},{6,8},{8,10},{10,12},{12,14},{14,16},{16,18},{18... | collective-permute-start | bytes 221192 | tf_op jit(solution)/shard_map/ppermute | solution.py:108
  1.2 11.8 %collective-permute-start.5 = (bf16[64,576]{1,0:T(8,128)(2,1)}, bf16[64,576]{1,0:T(8,128)(2,1)S(1)}, u32[]{:S(2)}, u32[]{:S(2)}) collective-permute-start(bf16[64,576]{1,0:T(8,128)(2,1)} %param.10), channel_id=1, source_target_pairs={{0,16},{2,18},{4,20},{6,22},{8,24},{10,26},{12,28},{14,30},{16,0},... | collective-permute-start | bytes 221192 | tf_op jit(solution)/shard_map/ppermute | solution.py:108
  4.8 9.7 %collective-permute-start.3 = (bf16[64,576]{1,0:T(8,128)(2,1)}, bf16[64,576]{1,0:T(8,128)(2,1)S(1)}, u32[]{:S(2)}, u32[]{:S(2)}) collective-permute-start(bf16[64,576]{1,0:T(8,128)(2,1)} %param.10), channel_id=1, source_target_pairs={{0,4},{2,6},{4,8},{6,10},{8,12},{10,14},{12,16},{14,18},{16,20},{1... | collective-permute-start | bytes 221192 | tf_op jit(solution)/shard_map/ppermute | solution.py:108
  6.3 8.7 %collective-permute-start = (bf16[64,576]{1,0:T(8,128)(2,1)}, bf16[64,576]{1,0:T(8,128)(2,1)S(1)}, u32[]{:S(2)}, u32[]{:S(2)}) collective-permute-start(bf16[64,576]{1,0:T(8,128)(2,1)} %param.10), channel_id=1, source_target_pairs={{0,1},{1,0},{2,3},{3,2},{4,5},{5,4},{6,7},{7,6},{8,9},{9,8},{10,11... | collective-permute-start | bytes 221192 | tf_op jit(solution)/shard_map/ppermute | solution.py:108
  7.8 13.4 %copy-start = (f32[128,32]{0,1:T(8,128)S(1)}, f32[128,32]{0,1:T(8,128)}, u32[]{:S(2)}) copy-start(f32[128,32]{0,1:T(8,128)} %param.8) | copy-start | bytes 49156
  7.9 13.4 %copy-start.1 = (f32[128,32]{0,1:T(8,128)S(1)}, f32[128,32]{0,1:T(8,128)}, u32[]{:S(2)}) copy-start(f32[128,32]{0,1:T(8,128)} %param.9) | copy-start | bytes 49156
  7.9 13.4 %copy-start.2 = (s32[1,4]{1,0:T(1,128)S(1)}, s32[1,4]{1,0:T(1,128)}, u32[]{:S(2)}) copy-start(s32[1,4]{1,0:T(1,128)} %links.1) | copy-start | bytes 52
  12.4 5.4 %collective-permute-start.2 = (bf16[64,576]{1,0:T(8,128)(2,1)S(1)}, bf16[64,576]{1,0:T(8,128)(2,1)S(1)}, u32[]{:S(2)}, u32[]{:S(2)}) collective-permute-start(bf16[64,576]{1,0:T(8,128)(2,1)S(1)} %collective-permute-done.1), channel_id=1, source_target_pairs={{0,1},{1,0},{2,3},{3,2},{4,5},{5,4},{6,7},{7,6},{8,9},{9,8},{10,11... | collective-permute-start | bytes 221192 | tf_op jit(solution)/shard_map/ppermute | solution.py:108
  13.0 6.6 %collective-permute-start.6 = (bf16[64,576]{1,0:T(8,128)(2,1)S(1)}, bf16[64,576]{1,0:T(8,128)(2,1)S(1)}, u32[]{:S(2)}, u32[]{:S(2)}) collective-permute-start(bf16[64,576]{1,0:T(8,128)(2,1)S(1)} %collective-permute-done.5), channel_id=1, source_target_pairs={{0,1},{1,0},{2,3},{3,2},{4,5},{5,4},{6,7},{7,6},{8,9},{9,8},{10,11... | collective-permute-start | bytes 221192 | tf_op jit(solution)/shard_map/ppermute | solution.py:108
  14.5 6.6 %collective-permute-start.4 = (bf16[64,576]{1,0:T(8,128)(2,1)S(1)}, bf16[64,576]{1,0:T(8,128)(2,1)S(1)}, u32[]{:S(2)}, u32[]{:S(2)}) collective-permute-start(bf16[64,576]{1,0:T(8,128)(2,1)S(1)} %collective-permute-done.3), channel_id=1, source_target_pairs={{0,1},{1,0},{2,3},{3,2},{4,5},{5,4},{6,7},{7,6},{8,9},{9,8},{10,11... | collective-permute-start | bytes 221192 | tf_op jit(solution)/shard_map/ppermute | solution.py:108
  40.1 9.5 %collective-permute-start.7 = (bf16[4,64,576]{2,1,0:T(8,128)(2,1)S(1)}, bf16[4,64,576]{2,1,0:T(8,128)(2,1)S(1)}, u32[]{:S(2)}, u32[]{:S(2)}) collective-permute-start(bf16[4,64,576]{2,1,0:T(8,128)(2,1)S(1)} %bitcast.46), channel_id=1, source_target_pairs={{0,1},{1,0},{2,3},{3,2},{4,5},{5,4},{6,7},{7,6},{8,9},{9,8},{10,11... | collective-permute-start | bytes 884744 | tf_op jit(solution)/shard_map/ppermute | solution.py:108
  49.8 3.8 %collective-permute-start.8 = (bf16[64,576]{1,0:T(8,128)(2,1)S(1)}, bf16[64,576]{1,0:T(8,128)(2,1)S(1)}, u32[]{:S(2)}, u32[]{:S(2)}) collective-permute-start(bf16[64,576]{1,0:T(8,128)(2,1)S(1)} %get-tuple-element.10), channel_id=1, source_target_pairs={{0,30},{2,0},{4,2},{6,4},{8,6},{10,8},{12,10},{14,12},{16,14},{18,... | collective-permute-start | bytes 221192 | tf_op jit(solution)/shard_map/ppermute | solution.py:108
  51.5 6.3 %collective-permute-start.10 = (bf16[64,576]{1,0:T(8,128)(2,1)S(1)}, bf16[64,576]{1,0:T(8,128)(2,1)S(1)}, u32[]{:S(2)}, u32[]{:S(2)}) collective-permute-start(bf16[64,576]{1,0:T(8,128)(2,1)S(1)} %get-tuple-element.11), channel_id=1, source_target_pairs={{0,16},{2,18},{4,20},{6,22},{8,24},{10,26},{12,28},{14,30},{16,0},... | collective-permute-start | bytes 221192 | tf_op jit(solution)/shard_map/ppermute | solution.py:108
  51.5 6.3 %collective-permute-start.9 = (bf16[64,576]{1,0:T(8,128)(2,1)S(1)}, bf16[64,576]{1,0:T(8,128)(2,1)S(1)}, u32[]{:S(2)}, u32[]{:S(2)}) collective-permute-start(bf16[64,576]{1,0:T(8,128)(2,1)S(1)} %get-tuple-element.12), channel_id=1, source_target_pairs={{0,28},{2,30},{4,0},{6,2},{8,4},{10,6},{12,8},{14,10},{16,12},{18,... | collective-permute-start | bytes 221192 | tf_op jit(solution)/shard_map/ppermute | solution.py:108
